TPU v7x, 256 devices: a whole 4x4x8 slice. The times are simulated.
256 devices in a mesh: blk: 16 (over y, z_lo, core), dp: 16 (over z_hi, x).
Axes of the slice: x: 4, y: 4, z: 8 (z_hi: 4, z_lo: 2; z = z_hi * 2 + z_lo), core: 2. Of those that a mesh axis runs over, the one named last changes fastest.
Arguments:
- queries: bfloat16 [32768, 256], P(('blk', 'dp')), may hold values from -30 to 30, as said below
- pois: bfloat16 [32768, 256], P(('blk', 'dp')), may hold values from -4 to 4, as said below
- query_region: int32 [32768], P(('blk', 'dp')), may hold values from 0 to 63
- block_region: int32 [256], P(('blk', 'dp')), may hold values from 0 to 63
- region_mask: int32 [64, 64], replicated, may hold values from 0 to 1
- positive: int32 [32768], P(('blk', 'dp')), may hold values from 0 to 32767
Outputs:
- loss: float32 [32768], P(('blk', 'dp'))
- query_grad: float32 [32768, 256], P(('blk', 'dp'))
- poi_grad: float32 [32768, 256], P(('blk', 'dp'))
Inputs may be any that keep to these rules, and one draw needn't show every extreme that they name: `queries`: float entries. `pois`: float entries.
All inputs are finite; a program needn't handle non-finite values.
Results may differ from a plain program's by a relative error of at most 0.00185.
Values may be sent and summed in bfloat16 or wider, within the bound.
A program may use at most 64 MiB of HBM per device.

v0:
```python
import math
import jax
import jax.numpy as jnp
from jax import lax
from jax.sharding import PartitionSpec as P

TILE = 128
floor_value = -1e30


def shifted(x, axis, by):
    length = lax.axis_size(axis)
    return lax.ppermute(x, axis, [(i, (i + by) % length) for i in range(length)])


def combined_all(x, axis, combine):
    everything = jax.tree.map(lambda part: lax.all_gather(part, axis), x)
    leading = jax.tree.map(lambda part: part[0], everything)

    def lap(k, so_far):
        return combine(so_far, jax.tree.map(lambda part: part[k], everything))

    return lax.fori_loop(1, lax.axis_size(axis), lap, leading)


def combine_parts(first, second):
    highest = jnp.maximum(first[0], second[0])
    total = first[1] * jnp.exp(first[0] - highest) + second[1] * jnp.exp(second[0] - highest)
    return (highest, total, first[2] + second[2])


def body(queries, pois, query_region, block_region, region_mask, positive):
    group_count = lax.axis_size("dp")
    cycle_count = lax.axis_size("blk")
    cycle_index = lax.axis_index("blk")
    group_index = lax.axis_index("dp")
    slab_rows = pois.shape[0]
    own_rows = queries.shape[0]
    width = queries.shape[1]
    regions = region_mask.shape[0]
    scale = 1.0 / math.sqrt(width)
    group_q = lax.all_gather(queries, "dp", axis=0, tiled=True)
    group_reg, group_pos = (
        lax.all_gather(query_region, "dp", axis=0, tiled=True),
        lax.all_gather(positive, "dp", axis=0, tiled=True),
    )
    block_all = lax.all_gather(block_region, ("blk", "dp"), axis=0, tiled=True)
    group_rows = group_q.shape[0]
    region_ids = jnp.arange(regions, dtype=jnp.int32)
    query_hot = (group_reg[:, None] == region_ids[None, :]).astype(jnp.bfloat16)
    block_hot = (block_all[:, None] == region_ids[None, :]).astype(jnp.bfloat16)
    mask_rows = jnp.dot(
        query_hot, region_mask.astype(jnp.bfloat16), preferred_element_type=jnp.float32
    ).astype(jnp.bfloat16)
    block_open = (
        lax.dot_general(
            mask_rows, block_hot, (((1,), (1,)), ((), ())), preferred_element_type=jnp.float32
        )
        > 0.5
    )
    pos_block = group_pos // TILE

    def anchor_start(anchor):
        return (anchor % cycle_count * group_count + group_index) * slab_rows

    def piece_masks(start, count):
        columns = start + jnp.arange(count, dtype=jnp.int32)
        blocks = columns // TILE
        opened = jnp.take(block_open, blocks, axis=1) | (blocks[None, :] == pos_block[:, None])
        is_pos = columns[None, :] == group_pos[:, None]
        return (opened, is_pos)

    def logits(slab):
        return (
            lax.dot_general(
                group_q, slab, (((1,), (1,)), ((), ())), preferred_element_type=jnp.float32
            )
            * scale
        )

    def forward_piece(state, slab, start):
        opened, is_pos = piece_masks(start, slab.shape[0])
        highest, total, pos_score = state
        scores = logits(slab)
        masked = jnp.where(opened, scores, floor_value)
        new_high = jnp.maximum(highest, jnp.max(masked, axis=1))
        total = total * jnp.exp(highest - new_high) + jnp.sum(
            jnp.where(opened, jnp.exp(scores - new_high[:, None]), 0.0), axis=1
        )
        pos_score = pos_score + jnp.sum(jnp.where(is_pos, scores, 0.0), axis=1)
        return (new_high, total, pos_score)

    def backward_piece(query_acc, slab, start, log_total):
        opened, is_pos = piece_masks(start, slab.shape[0])
        current = query_acc
        scores = logits(slab)
        weights = (
            jnp.where(opened, jnp.exp(scores - log_total[:, None]), 0.0)
            - is_pos.astype(jnp.float32)
        ).astype(jnp.bfloat16)
        current = current + jnp.dot(weights, slab, preferred_element_type=jnp.float32)
        tile_grad = lax.dot_general(
            weights, group_q, (((0,), (0,)), ((), ())), preferred_element_type=jnp.float32
        )
        return (current, tile_grad)

    initial = (
        jnp.full((group_rows,), floor_value, jnp.float32),
        jnp.zeros((group_rows,), jnp.float32),
        jnp.zeros((group_rows,), jnp.float32),
    )
    query_acc = jnp.zeros((group_rows, width), jnp.float32)
    state = forward_piece(initial, pois, anchor_start(cycle_index))

    def forward_step(step, carry):
        slab, current = carry
        slab = shifted(slab, "blk", 1)
        return (slab, forward_piece(current, slab, anchor_start(cycle_index - step)))

    unused, state = lax.fori_loop(1, cycle_count, forward_step, (pois, state))
    highest, total, pos_score = combined_all(state, "dp", combine_parts)
    log_total = highest + jnp.log(total)
    losses = log_total - pos_score
    loss = lax.dynamic_slice_in_dim(losses, group_index * own_rows, own_rows, 0)

    def backward_step(step, carry):
        slab, grads, current = carry
        current, tile_grad = backward_piece(
            current, slab, anchor_start(cycle_index - step), log_total
        )
        grads = grads + tile_grad
        slab = shifted(slab, "blk", 1)
        grads = shifted(grads, "blk", 1)
        return (slab, grads, current)

    start_grads = jnp.zeros((slab_rows, width), jnp.float32)
    unused, poi_sum, query_acc = lax.fori_loop(
        0, cycle_count, backward_step, (pois, start_grads, query_acc)
    )
    query_grad = lax.psum_scatter(query_acc * scale, "dp", scatter_dimension=0, tiled=True)
    return (loss, query_grad, poi_sum * scale)


def solution(mesh):
    in_specs = (
        P(("blk", "dp"), None),
        P(("blk", "dp"), None),
        P(("blk", "dp")),
        P(("blk", "dp")),
        P(),
        P(("blk", "dp")),
    )
    out_specs = (P(("blk", "dp")), P(("blk", "dp"), None), P(("blk", "dp"), None))
    return jax.shard_map(body, mesh=mesh, in_specs=in_specs, out_specs=out_specs, check_vma=False)
```

profile of v0, /device:TPU:8, one launch (start us, length us, event | category | flops | bytes accessed | tf_op | source)
XLA Modules:
  0.0 693.0 jit_solution(1324821323674346143)
XLA Ops:
  8.9 80.1 %all-reduce = s32[256]{0:T(256)S(1)} all-reduce(s32[256]{0:T(256)S(1)} %dynamic-update-slice), channel_id=1, replica_groups=mesh['blk'=16,'dp'=16] {'blk','dp'}, use_global_device_ids=true, to_apply=%add | all-reduce | flops 256 | bytes 2048
  89.1 41.1 %all-gather.3 = s32[16,1,128]{2,1,0:T(1,128)S(1)} all-gather(s32[1,1,128]{2,1,0:T(1,128)} %bitcast.66), channel_id=1, replica_groups=mesh['blk'=16,'dp'=16] {'dp'}, dimensions={0}, use_global_device_ids=true | all-gather | bytes 8704 | tf_op jit(solution)/shard_map/all_gather | solution.py:44
  134.5 37.8 %all-gather.4 = s32[16,1,128]{2,1,0:T(1,128)S(1)} all-gather(s32[1,1,128]{2,1,0:T(1,128)S(1)} %bitcast.67), channel_id=1, replica_groups=mesh['blk'=16,'dp'=16] {'dp'}, dimensions={0}, use_global_device_ids=true | all-gather | bytes 8704 | tf_op jit(solution)/shard_map/all_gather | solution.py:45
  172.3 1.8 select_reduce_fusion.5
  174.7 110.5 %while.60 = (s32[]{:T(128)}, bf16[128,256]{1,0:T(8,128)(2,1)S(1)}, f32[2048]{0:T(1024)S(1)}, f32[2048]{0:T(1024)S(1)}, f32[2048]{0:T(1024)S(1)}, /*index=5*/s32[...) while((s32[]{:T(128)}, bf16[128,256]{1,0:T(8,128)(2,1)S(1)}, ...), condition=%wide.region_7.9_spmd, body=%wide.region_3.8_spmd.sunk | while | flops 138162320 | bytes 4825830 | solution.py:120
  176.5 2.8 collective-permute-done
  179.4 1.8 select_reduce_fusion.8
  183.6 2.8 collective-permute-done
  190.8 2.8 collective-permute-done
  197.9 2.8 collective-permute-done
  200.7 1.8 select_reduce_fusion.8
  205.0 2.8 collective-permute-done
  207.8 1.8 select_reduce_fusion.8
  212.1 2.8 collective-permute-done
  219.2 2.8 collective-permute-done
  222.0 1.8 select_reduce_fusion.8
  226.3 2.8 collective-permute-done
  229.2 1.8 select_reduce_fusion.8
  233.4 2.8 collective-permute-done
  240.5 2.8 collective-permute-done
  243.4 1.8 select_reduce_fusion.8
  247.6 2.8 collective-permute-done
  250.5 1.8 select_reduce_fusion.8
  254.7 3.0 collective-permute-done
  262.0 4.1 collective-permute-done
  270.4 4.1 collective-permute-done
  278.7 4.1 collective-permute-done
  285.2 39.0 %all-gather = f32[32768]{0:T(1024)S(1)} all-gather(f32[2048]{0:T(1024)S(1)} %get-tuple-element.719), channel_id=2, replica_groups=mesh['blk'=16,'dp'=16] {'dp'}, dimensions={0}, use_global_device_ids=true | all-gather | bytes 139264 | tf_op jit(solution)/shard_map/all_gather | solution.py:17
  324.2 40.4 %all-gather.1 = f32[32768]{0:T(1024)S(1)} all-gather(f32[2048]{0:T(1024)S(1)} %get-tuple-element.720), channel_id=3, replica_groups=mesh['blk'=16,'dp'=16] {'dp'}, dimensions={0}, use_global_device_ids=true | all-gather | bytes 139264 | tf_op jit(solution)/shard_map/all_gather | solution.py:17
  364.6 39.2 %all-gather.2 = f32[32768]{0:T(1024)S(1)} all-gather(f32[2048]{0:T(1024)S(1)} %get-tuple-element.721), channel_id=4, replica_groups=mesh['blk'=16,'dp'=16] {'dp'}, dimensions={0}, use_global_device_ids=true | all-gather | bytes 139264 | tf_op jit(solution)/shard_map/all_gather | solution.py:17
  406.0 178.6 %while.62 = (s32[]{:T(128)}, bf16[128,256]{1,0:T(8,128)(2,1)S(1)}, f32[128,256]{1,0:T(8,128)S(1)}, f32[2048,256]{1,0:T(8,128)S(1)}, s32[]{:T(128)}, /*index=5*/s...) while((s32[]{:T(128)}, bf16[128,256]{1,0:T(8,128)(2,1)S(1)}, ...), condition=%wide.region_11.13_spmd.clone, body=%wide.region_10.12_spmd.clone.sunk | while | flops 406362368 | bytes 14713012 | solution.py:137
  408.3 2.2 fusion.39
  411.6 4.6 collective-permute-done.2
  418.3 2.2 fusion.39
  422.7 5.4 collective-permute-done.2
  430.2 2.2 fusion.39
  433.6 4.6 collective-permute-done.2
  440.2 2.2 fusion.39
  444.6 5.4 collective-permute-done.2
  452.1 2.2 fusion.39
  455.8 5.4 collective-permute-done.2
  463.3 2.2 fusion.39
  467.0 5.4 collective-permute-done.2
  474.6 2.2 fusion.39
  478.3 5.4 collective-permute-done.2
  485.8 2.2 fusion.39
  489.5 5.4 collective-permute-done.2
  497.0 2.2 fusion.39
  500.7 5.4 collective-permute-done.2
  508.2 2.2 fusion.39
  511.9 5.4 collective-permute-done.2
  519.4 2.2 fusion.39
  523.1 5.4 collective-permute-done.2
  530.6 2.2 fusion.39
  534.4 5.4 collective-permute-done.2
  541.9 2.2 fusion.39
  545.6 5.4 collective-permute-done.2
  553.1 2.2 fusion.39
  556.8 5.4 collective-permute-done.2
  564.3 2.2 fusion.39
  568.0 5.4 collective-permute-done.2
  575.5 2.2 fusion.39
  579.2 5.4 collective-permute-done.2
  588.1 98.1 %reduce-scatter.2.cloned.1.call-done = f32[128,256]{1,0:T(8,128)} async-done(((f32[2048,256]{1,0:T(8,128)}), f32[128,256]{1,0:T(8,128)}) %reduce-scatter.2.cloned.1.call-update) | async-done | bytes 131088 | tf_op jit(solution)/shard_map/reduce_scatter | solution.py:140
  (509 shorter events, 119.1 us)
Async XLA Ops:
  7.2 165.1 %all-gather.7.cloned.1.call-start = ((), (), s32[]{:S(2)}) async-start(), calls=%async_computation.1 | async-start | bytes 1114112 | tf_op jit(solution)/shard_map/all_gather | solution.py:42
  8.1 678.1 %reduce-scatter.2.cloned.1.call-start = ((), (), s32[]{:S(2)}) async-start(), calls=%async_computation.2 | async-start | bytes 2228224 | tf_op jit(solution)/shard_map/reduce_scatter | solution.py:140
  131.7 2.7 copy-start.2
  174.7 4.7 collective-permute-start
  181.8 4.7 collective-permute-start
  188.9 4.7 collective-permute-start
  196.0 4.7 collective-permute-start
  203.2 4.7 collective-permute-start
  210.3 4.7 collective-permute-start
  217.4 4.7 collective-permute-start
  224.5 4.7 collective-permute-start
  231.6 4.7 collective-permute-start
  238.7 4.7 collective-permute-start
  245.8 4.7 collective-permute-start
  252.9 4.9 collective-permute-start
  260.2 5.9 collective-permute-start
  268.5 5.9 collective-permute-start
  276.9 5.9 collective-permute-start
  406.1 5.5 collective-permute-start.1
  408.2 2.2 copy-start
  410.8 5.4 collective-permute-start.2
  416.2 6.6 collective-permute-start.1
  418.2 2.2 copy-start
  420.8 7.3 %collective-permute-start.2 = (f32[128,256]{1,0:T(8,128)S(1)}, f32[128,256]{1,0:T(8,128)S(1)}, u32[]{:S(2)}, u32[]{:S(2)}) collective-permute-start(f32[128,256]{1,0:T(8,128)S(1)} %convolution_add_fusion.4), channel_id=1, source_target_pairs={{0,16},{16,32},{32,48},{48,64},{64,80},{80,96},{96,112},{112,128},... | collective-permute-start | bytes 393224 | tf_op jit(solution)/shard_map/while/body/eval_jaxpr/ppermute | solution.py:13
  428.1 5.4 collective-permute-start.1
  430.2 2.2 copy-start
  432.8 5.4 collective-permute-start.2
  438.2 6.5 collective-permute-start.1
  440.2 2.2 copy-start
  442.8 7.2 %collective-permute-start.2 = (f32[128,256]{1,0:T(8,128)S(1)}, f32[128,256]{1,0:T(8,128)S(1)}, u32[]{:S(2)}, u32[]{:S(2)}) collective-permute-start(f32[128,256]{1,0:T(8,128)S(1)} %convolution_add_fusion.4), channel_id=1, source_target_pairs={{0,16},{16,32},{32,48},{48,64},{64,80},{80,96},{96,112},{112,128},... | collective-permute-start | bytes 393224 | tf_op jit(solution)/shard_map/while/body/eval_jaxpr/ppermute | solution.py:13
  450.0 5.8 collective-permute-start.1
  452.1 2.2 copy-start
  454.7 6.6 collective-permute-start.2
  461.2 5.8 collective-permute-start.1
  463.3 2.2 copy-start
  465.9 6.6 collective-permute-start.2
  472.5 5.8 collective-permute-start.1
  474.6 2.2 copy-start
  477.1 6.6 collective-permute-start.2
  483.7 5.8 collective-permute-start.1
  485.8 2.2 copy-start
  488.3 6.6 collective-permute-start.2
  494.9 5.8 collective-permute-start.1
  497.0 2.2 copy-start
  499.5 6.6 collective-permute-start.2
  506.1 5.8 collective-permute-start.1
  508.2 2.2 copy-start
  510.7 6.6 collective-permute-start.2
  517.3 5.8 collective-permute-start.1
  519.4 2.2 copy-start
  522.0 6.6 collective-permute-start.2
  528.5 5.8 collective-permute-start.1
  530.6 2.2 copy-start
  533.2 6.6 collective-permute-start.2
  539.8 5.8 collective-permute-start.1
  541.9 2.2 copy-start
  544.4 6.6 collective-permute-start.2
  551.0 5.8 collective-permute-start.1
  553.1 2.2 copy-start
  555.6 6.6 collective-permute-start.2
  562.2 5.8 collective-permute-start.1
  566.8 6.6 collective-permute-start.2
  573.4 5.8 collective-permute-start.1
  578.0 6.6 collective-permute-start.2
  (3 other events, 5.0 us)
Sparse Core Ops, SparseCore 0:
  10.4 56.3 all-gather.6
  586.3 99.8 reduce-scatter.1
where the time goes:
time: 694 us; the launch traced here: 693 us
  blocking collectives  278 us (40%)
  waiting for transfers between devices  236 us (34%)
  matrix products  81.3 us (12%)
  local copies, waits for them, and re-layouts  60.6 us (9%)
  other arithmetic  15.1 us (2%)
  between operations  14.9 us (2%)
    ppermute x47, waiting for transfers between devices, shifted(): lax.ppermute(x, axis, [(i, (i + by) % length) for i in range(length)])  138 us
    all_gather x3, blocking collectives, combined_all(): everything = jax.tree.map(lambda part: lax.all_gather(part, axis), x)  119 us
    reduce_scatter x1, waiting for transfers between devices, body(): lax.psum_scatter(query_acc * scale, 'dp', scatter_dimension=0, tiled=True)  98.1 us
    unnamed x1, blocking collectives  80.1 us
    dot_general x32, matrix products, logits(): lax.dot_general(group_q, slab, (((1,), (1,)), ((), ())), preferred_elemen...  63 us
    gather x48, local copies, waits for them, and re-layouts, piece_masks(): jnp.take(block_open, blocks, axis=1)  57.7 us
    all_gather x1, blocking collectives, body(): lax.all_gather(query_region, 'dp', axis=0, tiled=True)  41.1 us
    all_gather x1, blocking collectives, body(): lax.all_gather(positive, 'dp', axis=0, tiled=True)  37.8 us
  transfers between devices with their start and end apart: 49, of which 46 were waited for; matrix products, arithmetic and copies ran while one was open for 17% of the time, Pallas kernels for 0%

commit v1 on v0

--- a/solution.py
+++ b/solution.py
@@ -6,6 +6,13 @@
 
 TILE = 128
 floor_value = -1e30
+
+
+def all_by_exchange(array, mesh_axis, d):
+    count = lax.axis_size(mesh_axis)
+    pieces = jnp.stack([array for _ in range(count)])
+    pieces = lax.all_to_all(pieces, mesh_axis, split_axis=0, concat_axis=0)
+    return jnp.concatenate(pieces, axis=d)
 
 
 def shifted(x, axis, by):
@@ -42,7 +49,7 @@
     group_q = lax.all_gather(queries, "dp", axis=0, tiled=True)
     group_reg, group_pos = (
         lax.all_gather(query_region, "dp", axis=0, tiled=True),
-        lax.all_gather(positive, "dp", axis=0, tiled=True),
+        all_by_exchange(positive, "dp", 0),
     )
     block_all = lax.all_gather(block_region, ("blk", "dp"), axis=0, tiled=True)
     group_rows = group_q.shape[0]

time: 694 us -> 665 us (0.958)
  blocking collectives: 278 us -> 237 us
  starting transfers between devices: 2.78 us -> 13.8 us
    all_gather x1 -> x0, blocking collectives: 37.8 us -> none  [body(): lax.all_gather(positive, 'dp', axis=0, tiled=True)]
    all_to_all x0 -> x1, starting transfers between devices: none -> 11 us  [all_by_exchange(): pieces = lax.all_to_all(pieces, mesh_axis, split_axis=0, concat_axis=0)]
  transfers between devices with their start and end apart: 49 -> 50, of which waited for: 46 -> 46; matrix products, arithmetic and copies ran while one was open for 17% -> 18% of each run, Pallas kernels for 0% -> 0%
where the time goes in v1:
time: 665 us; the launch traced here: 664 us
  blocking collectives  237 us (36%)
  waiting for transfers between devices  235 us (35%)
  matrix products  81.3 us (12%)
  local copies, waits for them, and re-layouts  61.9 us (9%)
  other arithmetic  15.1 us (2%)
  between operations  14.9 us (2%)
  starting transfers between devices  13.8 us (2%)
    ppermute x47, waiting for transfers between devices, shifted(): lax.ppermute(x, axis, [(i, (i + by) % length) for i in range(length)])  137 us
    all_gather x3, blocking collectives, combined_all(): everything = jax.tree.map(lambda part: lax.all_gather(part, axis), x)  119 us
    reduce_scatter x1, waiting for transfers between devices, body(): lax.psum_scatter(query_acc * scale, 'dp', scatter_dimension=0, tiled=True)  98.2 us
    unnamed x1, blocking collectives  77.3 us
    dot_general x32, matrix products, logits(): lax.dot_general(group_q, slab, (((1,), (1,)), ((), ())), preferred_elemen...  63 us
    gather x48, local copies, waits for them, and re-layouts, piece_masks(): jnp.take(block_open, blocks, axis=1)  57.7 us
    all_gather x1, blocking collectives, body(): lax.all_gather(query_region, 'dp', axis=0, tiled=True)  40.6 us
  transfers between devices with their start and end apart: 50, of which 46 were waited for; matrix products, arithmetic and copies ran while one was open for 18% of the time, Pallas kernels for 0%

profile of v1, /device:TPU:8, one launch (start us, length us, event | category | flops | bytes accessed | tf_op | source)
XLA Modules:
  0.0 663.5 jit_solution(8499687813709630585)
XLA Ops:
  9.3 11.0 %all-to-all-start = ((s32[16,1,128]{2,1,0:T(1,128)}), s32[16,1,128]{2,1,0:T(1,128)S(1)}, u32[]{:S(2)}, u32[]{:S(2)}) async-start(s32[16,1,128]{2,1,0:T(1,128)} %stack.2), calls=%async_computation | async-start | bytes 16384 | tf_op jit(solution)/shard_map/all_to_all | solution.py:14
  21.2 77.3 %all-reduce = s32[256]{0:T(256)S(1)} all-reduce(s32[256]{0:T(256)S(1)} %dynamic-update-slice), channel_id=1, replica_groups=mesh['blk'=16,'dp'=16] {'blk','dp'}, use_global_device_ids=true, to_apply=%add | all-reduce | flops 256 | bytes 2048
  98.5 40.6 %all-gather.3 = s32[16,1,128]{2,1,0:T(1,128)S(1)} all-gather(s32[1,1,128]{2,1,0:T(1,128)} %bitcast.74), channel_id=1, replica_groups=mesh['blk'=16,'dp'=16] {'dp'}, dimensions={0}, use_global_device_ids=true | all-gather | bytes 8704 | tf_op jit(solution)/shard_map/all_gather | solution.py:51
  143.5 1.8 select_reduce_fusion.5
  145.9 109.5 %while.60 = (s32[]{:T(128)}, bf16[128,256]{1,0:T(8,128)(2,1)S(1)}, f32[2048]{0:T(1024)S(1)}, f32[2048]{0:T(1024)S(1)}, f32[2048]{0:T(1024)S(1)}, /*index=5*/s32[...) while((s32[]{:T(128)}, bf16[128,256]{1,0:T(8,128)(2,1)S(1)}, ...), condition=%wide.region_7.9_spmd, body=%wide.region_3.8_spmd.sunk | while | flops 138162320 | bytes 4825830 | solution.py:127
  147.7 2.8 collective-permute-done
  154.8 2.8 collective-permute-done
  161.9 2.8 collective-permute-done
  164.8 1.8 select_reduce_fusion.8
  169.0 2.8 collective-permute-done
  171.9 1.8 select_reduce_fusion.8
  176.2 2.8 collective-permute-done
  183.3 2.8 collective-permute-done
  186.1 1.8 select_reduce_fusion.8
  190.4 2.8 collective-permute-done
  193.2 1.8 select_reduce_fusion.8
  197.5 2.8 collective-permute-done
  204.6 2.8 collective-permute-done
  207.4 1.8 select_reduce_fusion.8
  211.7 2.8 collective-permute-done
  214.6 1.8 select_reduce_fusion.8
  218.8 2.8 collective-permute-done
  225.9 2.8 collective-permute-done
  228.8 1.8 select_reduce_fusion.8
  233.0 3.3 collective-permute-done
  240.6 4.1 collective-permute-done
  248.9 4.1 collective-permute-done
  255.4 39.4 %all-gather = f32[32768]{0:T(1024)S(1)} all-gather(f32[2048]{0:T(1024)S(1)} %get-tuple-element.719), channel_id=2, replica_groups=mesh['blk'=16,'dp'=16] {'dp'}, dimensions={0}, use_global_device_ids=true | all-gather | bytes 139264 | tf_op jit(solution)/shard_map/all_gather | solution.py:24
  294.9 40.0 %all-gather.1 = f32[32768]{0:T(1024)S(1)} all-gather(f32[2048]{0:T(1024)S(1)} %get-tuple-element.720), channel_id=3, replica_groups=mesh['blk'=16,'dp'=16] {'dp'}, dimensions={0}, use_global_device_ids=true | all-gather | bytes 139264 | tf_op jit(solution)/shard_map/all_gather | solution.py:24
  334.9 39.5 %all-gather.2 = f32[32768]{0:T(1024)S(1)} all-gather(f32[2048]{0:T(1024)S(1)} %get-tuple-element.721), channel_id=4, replica_groups=mesh['blk'=16,'dp'=16] {'dp'}, dimensions={0}, use_global_device_ids=true | all-gather | bytes 139264 | tf_op jit(solution)/shard_map/all_gather | solution.py:24
  376.7 178.4 %while.62 = (s32[]{:T(128)}, bf16[128,256]{1,0:T(8,128)(2,1)S(1)}, f32[128,256]{1,0:T(8,128)S(1)}, f32[2048,256]{1,0:T(8,128)S(1)}, s32[]{:T(128)}, /*index=5*/s...) while((s32[]{:T(128)}, bf16[128,256]{1,0:T(8,128)(2,1)S(1)}, ...), condition=%wide.region_11.13_spmd.clone, body=%wide.region_10.12_spmd.clone.sunk | while | flops 406362368 | bytes 14713012 | solution.py:144
  378.9 2.2 fusion.39
  382.2 4.6 collective-permute-done.2
  388.9 2.2 fusion.39
  393.3 5.4 collective-permute-done.2
  400.8 2.2 fusion.39
  404.2 4.5 collective-permute-done.2
  410.8 2.2 fusion.39
  415.0 5.4 collective-permute-done.2
  422.6 2.2 fusion.39
  426.3 5.4 collective-permute-done.2
  433.8 2.2 fusion.39
  437.5 5.4 collective-permute-done.2
  445.0 2.2 fusion.39
  448.7 5.4 collective-permute-done.2
  456.2 2.2 fusion.39
  459.9 5.4 collective-permute-done.2
  467.4 2.2 fusion.39
  471.1 5.4 collective-permute-done.2
  478.6 2.2 fusion.39
  482.4 5.4 collective-permute-done.2
  489.9 2.2 fusion.39
  493.6 5.4 collective-permute-done.2
  501.1 2.2 fusion.39
  504.8 5.4 collective-permute-done.2
  512.3 2.2 fusion.39
  516.0 5.4 collective-permute-done.2
  523.5 2.2 fusion.39
  527.2 5.4 collective-permute-done.2
  534.7 2.2 fusion.39
  538.4 5.4 collective-permute-done.2
  545.9 2.2 fusion.39
  549.7 5.4 collective-permute-done.2
  558.5 98.2 %reduce-scatter.2.cloned.1.call-done = f32[128,256]{1,0:T(8,128)} async-done(((f32[2048,256]{1,0:T(8,128)}), f32[128,256]{1,0:T(8,128)}) %reduce-scatter.2.cloned.1.call-update) | async-done | bytes 131088 | tf_op jit(solution)/shard_map/reduce_scatter | solution.py:147
  (509 shorter events, 120.2 us)
Async XLA Ops:
  7.2 136.3 %all-gather.6.cloned.1.call-start = ((), (), s32[]{:S(2)}) async-start(), calls=%async_computation.2 | async-start | bytes 1114112 | tf_op jit(solution)/shard_map/all_gather | solution.py:49
  9.3 134.1 %all-to-all-start = ((s32[16,1,128]{2,1,0:T(1,128)}), s32[16,1,128]{2,1,0:T(1,128)S(1)}, u32[]{:S(2)}, u32[]{:S(2)}) async-start(s32[16,1,128]{2,1,0:T(1,128)} %stack.2), calls=%async_computation | async-start | bytes 16384 | tf_op jit(solution)/shard_map/all_to_all | solution.py:14
  20.4 636.3 %reduce-scatter.2.cloned.1.call-start = ((), (), s32[]{:S(2)}) async-start(), calls=%async_computation.3 | async-start | bytes 2228224 | tf_op jit(solution)/shard_map/reduce_scatter | solution.py:147
  145.9 4.7 collective-permute-start
  153.0 4.7 collective-permute-start
  160.1 4.7 collective-permute-start
  167.2 4.7 collective-permute-start
  174.3 4.7 collective-permute-start
  181.4 4.7 collective-permute-start
  188.6 4.7 collective-permute-start
  195.7 4.7 collective-permute-start
  202.8 4.7 collective-permute-start
  209.9 4.7 collective-permute-start
  217.0 4.7 collective-permute-start
  224.1 4.7 collective-permute-start
  231.2 5.1 collective-permute-start
  238.8 5.9 collective-permute-start
  247.1 5.9 collective-permute-start
  376.7 5.5 collective-permute-start.1
  378.9 2.2 copy-start
  381.4 5.4 collective-permute-start.2
  386.8 6.5 collective-permute-start.1
  388.9 2.2 copy-start
  391.4 7.3 %collective-permute-start.2 = (f32[128,256]{1,0:T(8,128)S(1)}, f32[128,256]{1,0:T(8,128)S(1)}, u32[]{:S(2)}, u32[]{:S(2)}) collective-permute-start(f32[128,256]{1,0:T(8,128)S(1)} %convolution_add_fusion.4), channel_id=1, source_target_pairs={{0,16},{16,32},{32,48},{48,64},{64,80},{80,96},{96,112},{112,128},... | collective-permute-start | bytes 393224 | tf_op jit(solution)/shard_map/while/body/eval_jaxpr/ppermute | solution.py:20
  398.7 5.4 collective-permute-start.1
  400.8 2.2 copy-start
  403.3 5.4 collective-permute-start.2
  408.7 6.3 collective-permute-start.1
  410.8 2.2 copy-start
  413.3 7.1 %collective-permute-start.2 = (f32[128,256]{1,0:T(8,128)S(1)}, f32[128,256]{1,0:T(8,128)S(1)}, u32[]{:S(2)}, u32[]{:S(2)}) collective-permute-start(f32[128,256]{1,0:T(8,128)S(1)} %convolution_add_fusion.4), channel_id=1, source_target_pairs={{0,16},{16,32},{32,48},{48,64},{64,80},{80,96},{96,112},{112,128},... | collective-permute-start | bytes 393224 | tf_op jit(solution)/shard_map/while/body/eval_jaxpr/ppermute | solution.py:20
  420.5 5.8 collective-permute-start.1
  422.6 2.2 copy-start
  425.1 6.6 collective-permute-start.2
  431.7 5.8 collective-permute-start.1
  433.8 2.2 copy-start
  436.3 6.6 collective-permute-start.2
  442.9 5.8 collective-permute-start.1
  445.0 2.2 copy-start
  447.5 6.6 collective-permute-start.2
  454.1 5.8 collective-permute-start.1
  456.2 2.2 copy-start
  458.7 6.6 collective-permute-start.2
  465.3 5.8 collective-permute-start.1
  467.4 2.2 copy-start
  470.0 6.6 collective-permute-start.2
  476.6 5.8 collective-permute-start.1
  478.6 2.2 copy-start
  481.2 6.6 collective-permute-start.2
  487.8 5.8 collective-permute-start.1
  489.9 2.2 copy-start
  492.4 6.6 collective-permute-start.2
  499.0 5.8 collective-permute-start.1
  501.1 2.2 copy-start
  503.6 6.6 collective-permute-start.2
  510.2 5.8 collective-permute-start.1
  512.3 2.2 copy-start
  514.8 6.6 collective-permute-start.2
  521.4 5.8 collective-permute-start.1
  523.5 2.2 copy-start
  526.0 6.6 collective-permute-start.2
  532.6 5.8 collective-permute-start.1
  537.3 6.6 collective-permute-start.2
  543.9 5.8 collective-permute-start.1
  548.5 6.6 collective-permute-start.2
  (3 other events, 5.0 us)
Sparse Core Ops, SparseCore 0:
  10.4 55.9 all-gather.5
  556.7 99.9 reduce-scatter.1
